TPU v7x, 32 devices: a whole 2x2x4 slice. The times are simulated.
32 devices in a mesh: seq: 8 (over y, x, core), tp: 4 (over z).
Axes of the slice: x: 2, y: 2, z: 4, core: 2. Of those that a mesh axis runs over, the one named last changes fastest.
Arguments:
- conv_values: bfloat16 [2048, 8192], P('seq', 'tp'), may hold values from -6 to 6
- gate_values: bfloat16 [2048, 8192], P('seq', 'tp'), may hold values from -6 to 6
- conv_maps: bfloat16 [2048, 2048], P('seq'), may hold values from -6 to 6
- step_raw: float32 [2048, 128], P('seq', 'tp'), may hold values from -8 to 13
- decay_log: float32 [128], P('tp'), may hold values from -20 to 2
- skip_gain: float32 [128], P('tp'), may hold values from 0.5 to 1.5
- values_kernel: float32 [4, 8192], P(None, 'tp'), may hold values from -3 to 3
- values_offset: float32 [8192], P('tp'), may hold values from -0.5 to 0.5
- maps_kernel: float32 [4, 2048], replicated, may hold values from -3 to 3
- maps_offset: float32 [2048], replicated, may hold values from -0.5 to 0.5
- norm_weight: float32 [8192], P('tp'), may hold values from 0.5 to 1.5
- out_weight: bfloat16 [8192, 8192], P('tp', 'seq'), may hold values from -0.0625 to 0.0625
- residual: bfloat16 [2048, 8192], P(('seq', 'tp')), may hold values from -6 to 6
Outputs:
- mixed: float32 [2048, 8192], P(('seq', 'tp'))
All inputs are finite; a program needn't handle non-finite values.
Results may differ from a plain program's by a relative error of at most 0.012.
Values may be sent and summed in bfloat16 or wider, within the bound.
A program may use at most 128 MiB of HBM per device.

v0:
```python
import jax
import jax.numpy as jnp
from jax import lax
from jax.sharding import PartitionSpec as P

HEADS = 128
HEAD_DIM = 64
STATE = 128
GROUPS = 8
CONV = 4


def passed_along(array, axis, by):
    size = lax.axis_size(axis)
    pairs = [(i, i + by) for i in range(size) if 0 <= i + by < size]
    return lax.ppermute(array, axis, pairs)


def entering_2(value, axis, join, neutral):
    count, mine = (lax.axis_size(axis), lax.axis_index(axis))
    pieces = jax.tree.map(lambda part: lax.all_gather(part, axis), value)
    subtotal = jax.tree.map(
        lambda part, zero: jnp.full_like(part, 0) + jnp.asarray(zero, part.dtype), value, neutral
    )

    def turn(position, subtotal):
        longer = join(subtotal, jax.tree.map(lambda part: part[position], pieces))
        return jax.tree.map(lambda new, old: jnp.where(position < mine, new, old), longer, subtotal)

    return lax.fori_loop(0, count - 1, turn, subtotal)


def rim_conv(rim_rows, local_rows, kernel, offset):
    length = local_rows.shape[0]
    padded = jnp.concatenate([rim_rows.astype(jnp.float32), local_rows.astype(jnp.float32)], axis=0)
    summed = offset[None, :] + kernel[0][None, :] * padded[0:length]
    for position in range(1, CONV):
        summed = summed + kernel[position][None, :] * padded[position : position + length]
    return jax.nn.silu(summed).astype(jnp.bfloat16)


def shards(
    conv_values,
    gate_values,
    conv_maps,
    step_raw,
    decay_log,
    skip_gain,
    values_kernel,
    values_offset,
    maps_kernel,
    maps_offset,
    norm_weight,
    out_weight,
    residual,
):
    highest = lax.Precision.HIGHEST
    length = conv_values.shape[0]
    heads_dev = decay_log.shape[0]
    rim_count = CONV - 1
    rim_inner, rim_maps = passed_along(
        (conv_values[length - rim_count :], conv_maps[length - rim_count :]), "seq", 1
    )
    values_conv = rim_conv(rim_inner, conv_values, values_kernel, values_offset)
    maps_conv = rim_conv(rim_maps, conv_maps, maps_kernel, maps_offset)
    step_size = jax.nn.softplus(step_raw)
    log_decay = -jnp.exp(decay_log)[None, :] * step_size
    cum_log = jnp.cumsum(log_decay, axis=0)
    heads_here = lax.axis_index("tp") * heads_dev + jnp.arange(heads_dev, dtype=jnp.int32)
    group_of = heads_here * GROUPS // HEADS
    one_hot = (group_of[:, None] == jnp.arange(GROUPS, dtype=jnp.int32)[None, :]).astype(
        jnp.float32
    )
    input_groups = maps_conv[:, : GROUPS * STATE].astype(jnp.float32).reshape(length, GROUPS, STATE)
    output_groups = (
        maps_conv[:, GROUPS * STATE :].astype(jnp.float32).reshape(length, GROUPS, STATE)
    )
    input_heads = jnp.einsum("hg,qgn->qhn", one_hot, input_groups, precision=highest)
    output_heads = jnp.einsum("hg,qgn->qhn", one_hot, output_groups, precision=highest)
    value_heads = values_conv.astype(jnp.float32).reshape(length, heads_dev, HEAD_DIM)
    causal = jnp.tril(jnp.ones((length, length), dtype=bool))
    gap_log = cum_log.T[:, :, None] - cum_log.T[:, None, :]
    kernel = jnp.where(causal[None], jnp.exp(jnp.where(causal[None], gap_log, 0.0)), 0.0)
    scores = jnp.einsum("thn,shn->hts", output_heads, input_heads, precision=highest)
    mixing = kernel * scores * step_size.T[:, None, :]
    within = jnp.einsum("hts,shp->thp", mixing, value_heads, precision=highest)
    end_weight = jnp.exp(cum_log[-1][None, :] - cum_log) * step_size
    local_state = jnp.einsum(
        "shp,shn->hpn", value_heads * end_weight[:, :, None], input_heads, precision=highest
    )
    shard_decay = jnp.exp(cum_log[-1])
    zeros_state = jnp.zeros_like(local_state)

    def combine(earlier, latter):
        return (earlier[0] * latter[0], latter[0][:, None, None] * earlier[1] + latter[1])

    prefix = entering_2(
        (shard_decay, local_state), "seq", combine, (jnp.ones_like(shard_decay), zeros_state)
    )
    entering = prefix[1]
    carried = (
        jnp.einsum("thn,hpn->thp", output_heads, entering, precision=highest)
        * jnp.exp(cum_log)[:, :, None]
    )
    mixer_out = within + carried + skip_gain[None, :, None] * value_heads
    gated_out = mixer_out * jax.nn.silu(gate_values.astype(jnp.float32)).reshape(
        length, heads_dev, HEAD_DIM
    )
    head_squares = jnp.sum(gated_out * gated_out, axis=2)
    all_heads = lax.all_gather(head_squares, "tp", axis=1, tiled=True)
    group_totals = jnp.sum(all_heads.reshape(length, GROUPS, HEADS // GROUPS), axis=2)
    group_squares = jnp.einsum("qg,hg->qh", group_totals, one_hot, precision=highest)
    inv_rms = lax.rsqrt(group_squares / (HEADS // GROUPS * HEAD_DIM) + 1e-05)
    normed = (
        (gated_out * inv_rms[:, :, None]).reshape(length, heads_dev * HEAD_DIM)
        * norm_weight[None, :]
    ).astype(jnp.bfloat16)
    weight_full = lax.all_gather(out_weight, "seq", axis=1, tiled=True)
    summed = lax.psum_scatter(
        jnp.dot(normed, weight_full, preferred_element_type=jnp.float32).astype(jnp.bfloat16),
        "tp",
        scatter_dimension=0,
        tiled=True,
    ).astype(jnp.float32)
    return residual.astype(jnp.float32) + summed


def solution(mesh):
    placed = (
        P("seq", "tp"),
        P("seq", "tp"),
        P("seq", None),
        P("seq", "tp"),
        P("tp"),
        P("tp"),
        P(None, "tp"),
        P("tp"),
        P(),
        P(),
        P("tp"),
        P("tp", "seq"),
        P(("seq", "tp"), None),
    )
    return jax.shard_map(
        shards, mesh=mesh, in_specs=placed, out_specs=P(("seq", "tp"), None), check_vma=False
    )
```

profile of v0, /device:TPU:0, one launch (start us, length us, event | category | flops | bytes accessed | tf_op | source)
XLA Modules:
  0.0 355.8 jit_solution(9589444797217661076)
XLA Ops:
  6.5 0.9 slice.75
  7.4 2.4 collective-permute-start.1
  9.8 0.8 slice.65
  10.6 4.5 %collective-permute-start = (bf16[3,2048]{1,0:T(4,128)(2,1)S(1)}, bf16[3,2048]{1,0:T(4,128)(2,1)S(1)}, u32[]{:S(2)}, u32[]{:S(2)}) collective-permute-start(bf16[3,2048]{1,0:T(4,128)(2,1)S(1)} %slice.65), channel_id=1, source_target_pairs={{0,4},{4,8},{8,12},{12,16},{16,20},{20,24},{24,28},{1,5},{5,9},{9,... | collective-permute-start | bytes 36872 | tf_op jit(solution)/shard_map/ppermute | solution.py:16
  15.1 0.9 fusion.59
  16.0 0.7 exponential_negate_fusion
  16.7 0.8 copy_bitcast_fusion.1
  17.5 0.6 reduce-window.6
  18.6 0.9 bitcast_exponential_fusion
  19.4 0.9 fusion.60
  20.4 1.5 convert_element_type.42
  21.9 0.2 convert_element_type.39
  22.2 0.4 copy-done.8
  22.6 1.4 multiply_convert_fusion
  24.0 0.9 slice_bitcast_fusion.1
  25.0 1.4 multiply_convert_fusion.1
  26.4 0.5 copy.25
  27.0 0.7 convolution_bitcast_fusion
  27.9 1.7 copy-done.1
  29.7 6.0 %fusion.13 = f32[32,64,128]{2,1,0:T(8,128)} fusion(f32[256,32,128]{2,1,0:T(8,128)S(1)} %convolution_bitcast_fusion, bf16[256,32,64]{0,2,1:T(8,128)(2,1)S(1)} %bitcast.82, f32[256,32]{0,1:T(8,128)S(1)} %get-tuple-element.133), kind=kOutput, calls=%fused_computation.16 | convolution fusion | flops 806354944 | bytes 6324224 | tf_op jit(solution)/shard_map/shp,shn->hpn/dot_general | solution.py:88
  35.7 0.7 all-gather.5.cloned.1.call-update
  36.5 1.8 convert_multiply_fusion
  38.3 1.8 copy.32
  40.1 8.8 %all-gather.1 = f32[8,1,32]{2,1,0:T(1,128)S(1)} all-gather(f32[1,1,32]{2,1,0:T(1,128)S(1)} %bitcast.97), channel_id=1, replica_groups=mesh['seq'=8,'tp'=4] {'seq'}, dimensions={0}, use_global_device_ids=true | all-gather | bytes 1152 | tf_op jit(solution)/shard_map/all_gather | solution.py:21
  48.9 1.1 copy.35
  50.1 0.7 convolution_bitcast_fusion.1
  50.8 2.0 copy-done
  52.9 0.6 copy-done.2
  53.5 16.3 %fusion.15 = f32[32,256,256]{2,1,0:T(8,128)} fusion(f32[256,32,128]{2,1,0:T(8,128)S(1)} %copy-done.2, f32[256,32,128]{2,1,0:T(8,128)S(1)} %convolution_bitcast_fusion.1), kind=kOutput, calls=%fused_computation.18 | convolution fusion | flops 3221225472 | bytes 16777216 | tf_op jit(solution)/shard_map/thn,shn->hts/dot_general | solution.py:84
  69.8 20.7 %all-gather.7.cloned.1.call-done = f32[256,64,128]{2,1,0:T(8,128)} async-done(((f32[32,64,128]{2,1,0:T(8,128)}), f32[256,64,128]{2,1,0:T(8,128)}) %all-gather.7.cloned.1.call-update) | async-done | bytes 8388624 | tf_op jit(solution)/shard_map/all_gather | solution.py:21
  90.4 11.0 %while.14 = (s32[]{:T(128)}, f32[32,64,128]{2,1,0:T(8,128)S(1)}, s32[]{:T(128)}, f32[8,32]{1,0:T(8,128)S(1)}, f32[8,32,64,128]{3,2,1,0:T(8,128)}, /*index=5*/s32[]{:T(128)}, s32[]{:T(128)}) while((s32[]{:T(128)}, f32[32,64,128]{2,1,0:T(8,128)S(1)}, s32[]{:T(128)}, f32[8,32]{1,0:T(8,128)S(1)}, f32[8,32,64,128]{3,2,1,0:T(8,128)}, ...), condition=%wide.region_3.4_spmd.clone, body=%wide.region_2.3_spmd.clone.sunk | while | flops 1048580 | bytes 3146217 | solution.py:30
  90.4 1.5 fusion.69
  91.9 1.5 fusion.69
  93.4 1.5 fusion.69
  94.9 1.5 fusion.69
  96.4 1.5 fusion.69
  97.9 1.7 fusion.69
  99.7 1.7 fusion.69
  101.5 8.4 %fusion.17 = f32[32,64,256]{2,1,0:T(8,128)S(1)} fusion(f32[32,64,128]{2,1,0:T(8,128)S(1)} %get-tuple-element.99, f32[256,32,128]{2,1,0:T(8,128)} %copy-done), kind=kOutput, calls=%fused_computation.20 | convolution fusion | flops 805306368 | bytes 7340032 | tf_op jit(solution)/shard_map/thn,hpn->thp/dot_general | solution.py:102
  109.9 9.1 %multiply_reduce_fusion = (f32[256,32]{0,1:T(8,128)S(1)}, f32[256,32,64]{0,2,1:T(8,128)S(1)}) fusion(f32[256,32,64]{0,2,1:T(8,128)S(1)} %bitcast.87, bf16[256,32,64]{0,2,1:T(8,128)(2,1)S(1)} %bitcast.83, f32[32]{0:T(128)S(1)} %copy-done.11, f32[256,32]{0,1:T(8,128)S(1)} %get-tuple-element.132, f32[32,64,256]{2,1,0:T(8,128)S(1)} %fusion.17, ...), kind=kOutput, calls=%fused_computation.63 | convolution fusion | flops 1625284608 | bytes 15925376 | tf_op jit(solution)/shard_map/hts,shp->thp/dot_general | solution.py:86
  119.0 13.6 %all_gather.19 = f32[256,128]{0,1:T(8,128)S(1)} all-gather(f32[256,32]{0,1:T(8,128)S(1)} %get-tuple-element.145), channel_id=1, replica_groups=mesh['seq'=8,'tp'=4] {'tp'}, dimensions={1}, use_global_device_ids=true | all-gather | bytes 163840 | tf_op jit(solution)/shard_map/all_gather | solution.py:110
  132.9 0.2 broadcast_multiply_fusion
  133.1 0.5 copy-done.10
  133.6 0.3 fusion.43
  133.9 119.1 %all-gather.5.cloned.1.call-done = bf16[2048,8192]{1,0:T(8,128)(2,1)} async-done(((bf16[2048,1024]{1,0:T(8,128)(2,1)}), bf16[2048,8192]{1,0:T(8,128)(2,1)}) %all-gather.5.cloned.1.call-update) | async-done | bytes 33554448 | tf_op jit(solution)/shard_map/all_gather | solution.py:118
  253.0 16.5 %convolution_convert_fusion = bf16[256,8192]{1,0:T(8,128)(2,1)} fusion(bf16[256,2048]{0,1:T(8,128)(2,1)S(1)} %fusion.43, bf16[2048,8192]{1,0:T(8,128)(2,1)} %all-gather.5.cloned.1.call-done), kind=kOutput, calls=%fused_computation.3 | convolution fusion | flops 8592031744 | bytes 38797312 | tf_op jit(solution)/shard_map/dot_general | solution.py:120
  269.5 77.0 %reduce-scatter.2.cloned.1.call-done = bf16[64,8192]{1,0:T(8,128)(2,1)} async-done(((bf16[256,8192]{1,0:T(8,128)(2,1)}), bf16[64,8192]{1,0:T(8,128)(2,1)}) %reduce-scatter.2.cloned.1.call-update) | async-done | bytes 1048592 | tf_op jit(solution)/shard_map/reduce_scatter | solution.py:119
  346.5 2.7 convert_add_fusion
  (46 shorter events, 1.3 us)
Async XLA Ops:
  6.5 15.3 %copy-start.6 = (bf16[256,2048]{1,0:T(8,128)(2,1)S(1)}, bf16[256,2048]{1,0:T(8,128)(2,1)}, u32[]{:S(2)}) copy-start(bf16[256,2048]{1,0:T(8,128)(2,1)} %param.15) | copy-start | bytes 3145732
  6.5 83.9 %all-gather.7.cloned.1.call-start = ((), (), s32[]{:S(2)}) async-start(), calls=%async_computation.3 | async-start | bytes 9437184 | tf_op jit(solution)/shard_map/all_gather | solution.py:21
  7.4 14.7 %collective-permute-start.1 = (bf16[3,2048]{1,0:T(4,128)(2,1)S(1)}, bf16[3,2048]{1,0:T(4,128)(2,1)S(1)}, u32[]{:S(2)}, u32[]{:S(2)}) collective-permute-start(bf16[3,2048]{1,0:T(4,128)(2,1)S(1)} %slice.75), channel_id=1, source_target_pairs={{0,4},{4,8},{8,12},{12,16},{16,20},{20,24},{24,28},{1,5},{5,9},{9,... | collective-permute-start | bytes 36872 | tf_op jit(solution)/shard_map/ppermute | solution.py:16
  10.6 14.4 %collective-permute-start = (bf16[3,2048]{1,0:T(4,128)(2,1)S(1)}, bf16[3,2048]{1,0:T(4,128)(2,1)S(1)}, u32[]{:S(2)}, u32[]{:S(2)}) collective-permute-start(bf16[3,2048]{1,0:T(4,128)(2,1)S(1)} %slice.65), channel_id=1, source_target_pairs={{0,4},{4,8},{8,12},{12,16},{16,20},{20,24},{24,28},{1,5},{5,9},{9,... | collective-permute-start | bytes 36872 | tf_op jit(solution)/shard_map/ppermute | solution.py:16
  21.9 0.7 copy-start.8
  24.0 1.0 copy-start.9
  27.0 1.0 copy-start.3
  27.7 1.9 copy-start.1
  35.7 217.3 %all-gather.5.cloned.1.call-start = ((), (), s32[]{:S(2)}) async-start(), calls=%async_computation.1 | async-start | bytes 37748736 | tf_op jit(solution)/shard_map/all_gather | solution.py:118
  36.5 310.0 %reduce-scatter.2.cloned.1.call-start = ((), (), s32[]{:S(2)}) async-start(), calls=%async_computation.2 | async-start | bytes 5242880 | tf_op jit(solution)/shard_map/reduce_scatter | solution.py:119
  50.1 3.4 copy-start.2
  50.8 2.1 copy-start
  101.4 8.4 %copy-start.4 = (bf16[256,2048]{0,1:T(8,128)(2,1)S(1)}, bf16[256,2048]{0,1:T(8,128)(2,1)}, u32[]{:S(2)}) copy-start(bf16[256,2048]{0,1:T(8,128)(2,1)} %copy-done.3) | copy-start | bytes 3145732
  101.4 8.4 %copy-start.5 = (f32[256,2048]{0,1:T(8,128)S(1)}, f32[256,2048]{0,1:T(8,128)}, u32[]{:S(2)}) copy-start(f32[256,2048]{0,1:T(8,128)} %copy.32) | copy-start | bytes 6291460
  101.4 8.4 %copy-start.11 = (f32[32]{0:T(128)S(1)}, f32[32]{0:T(128)}, u32[]{:S(2)}) copy-start(f32[32]{0:T(128)} %param.20) | copy-start | bytes 388
  132.9 0.7 copy-start.10
  269.5 77.0 %copy-start.7 = (bf16[64,8192]{1,0:T(8,128)(2,1)S(1)}, bf16[64,8192]{1,0:T(8,128)(2,1)}, u32[]{:S(2)}) copy-start(bf16[64,8192]{1,0:T(8,128)(2,1)} %param.27) | copy-start | bytes 3145732
Sparse Core Ops, SparseCore 0:
  35.8 54.5 all-gather.6
  92.3 160.6 all-gather.4
  269.6 76.7 reduce-scatter.1
where the time goes:
time: 357 us; the launch traced here: 356 us
  waiting for transfers between devices  217 us (61%)
  matrix products  58 us (16%)
  other arithmetic  23.4 us (7%)
  blocking collectives  22.4 us (6%)
  local copies, waits for them, and re-layouts  13.9 us (4%)
  between operations  13.5 us (4%)
  starting transfers between devices  6.98 us (2%)
    all_gather x1, waiting for transfers between devices, shards(): weight_full = lax.all_gather(out_weight, 'seq', axis=1, tiled=True)  119 us
    reduce_scatter x1, waiting for transfers between devices, shards(): lax.psum_scatter(jnp.dot(normed, weight_full, preferred_element_type=jnp....  77 us
    all_gather x1, waiting for transfers between devices, entering_2(): pieces = jax.tree.map(lambda part: lax.all_gather(part, axis), value)  20.7 us
    dot_general x1, matrix products, shards(): jnp.dot(normed, weight_full, preferred_element_type=jnp.float32)  16.5 us
    dot_general x1, matrix products, shards(): jnp.einsum('thn,shn->hts', output_heads, input_heads, precision=highest)  16.3 us
    all_gather x1, blocking collectives, shards(): all_heads = lax.all_gather(head_squares, 'tp', axis=1, tiled=True)  13.6 us
    select_n x7, other arithmetic, turn(): jnp.where(position < mine, new, old)  10.7 us
    dot_general x1, matrix products, shards(): within = jnp.einsum('hts,shp->thp', mixing, value_heads, precision=highest)  9.09 us
  transfers between devices with their start and end apart: 5, of which 3 were waited for; matrix products, arithmetic and copies ran while one was open for 17% of the time, Pallas kernels for 0%

commit v1 on v0

--- a/solution.py
+++ b/solution.py
@@ -1,6 +1,10 @@
+import functools
+
 import jax
 import jax.numpy as jnp
 from jax import lax
+from jax.experimental import pallas as pl
+from jax.experimental.pallas import tpu as pltpu
 from jax.sharding import PartitionSpec as P
 
 HEADS = 128
@@ -37,6 +41,259 @@
     for position in range(1, CONV):
         summed = summed + kernel[position][None, :] * padded[position : position + length]
     return jax.nn.silu(summed).astype(jnp.bfloat16)
+
+
+def ring_place(spot, size):
+    if size % 4:
+        return spot
+    half = size // 2
+    past = spot - half
+    turned = half + (half - 2 - 2 * lax.div(past, 2)) + lax.rem(past, 2)
+    return jnp.where(spot < half, spot, turned)
+
+
+def mix_kernel(
+    n, m, x_ref, w_ref, out_ref, gat, part, up, down,
+    own_sem, gat_send, gat_recv, up_send, up_recv, down_send, down_recv, out_send, out_recv,
+):
+    mesh_ids = pl.DeviceIdType.MESH
+    me, z = lax.axis_index("seq"), lax.axis_index("tp")
+    spot = ring_place(me, n)
+    right = ring_place(lax.rem(spot + 1, n), n)
+    left = ring_place(lax.rem(spot + n - 1, n), n)
+    half = gat.shape[2]
+    depth = gat.shape[3]
+    width = w_ref.shape[1]
+    rows = part.shape[1] // m
+    tile = min(width, 256)
+
+    own = [
+        pltpu.make_async_copy(x_ref.at[pl.ds(d * half, half)], gat.at[0, d], own_sem.at[d])
+        for d in range(2)
+    ]
+    for copy in own:
+        copy.start()
+
+    barrier = pltpu.get_barrier_semaphore()
+
+    def greet(step, carry):
+        pl.semaphore_signal(
+            barrier, inc=1, device_id=(lax.rem(me + step, n), z), device_id_type=mesh_ids
+        )
+        return carry
+
+    lax.fori_loop(1, n, greet, 0)
+
+    @pl.when(z > 0)
+    def _():
+        pl.semaphore_signal(barrier, inc=1, device_id=(me, z - 1), device_id_type=mesh_ids)
+
+    @pl.when(z < m - 1)
+    def _():
+        pl.semaphore_signal(barrier, inc=1, device_id=(me, z + 1), device_id_type=mesh_ids)
+
+    beside = (z > 0).astype(jnp.int32) + (z < m - 1).astype(jnp.int32)
+    pl.semaphore_wait(barrier, n - 1 + beside)
+
+    for copy in own:
+        copy.wait()
+
+    def gather_copy(step, d):
+        return pltpu.make_async_remote_copy(
+            src_ref=gat.at[step, d],
+            dst_ref=gat.at[step + 1, d],
+            send_sem=gat_send.at[step, d],
+            recv_sem=gat_recv.at[step + 1, d],
+            device_id=(right if d == 0 else left, z),
+            device_id_type=mesh_ids,
+        )
+
+    def gather_arrival(step, d):
+        return pltpu.make_async_remote_copy(
+            src_ref=gat.at[step, d],
+            dst_ref=gat.at[step, d],
+            send_sem=gat_send.at[step, d],
+            recv_sem=gat_recv.at[step, d],
+            device_id=(right if d == 0 else left, z),
+            device_id_type=mesh_ids,
+        )
+
+    def chain_copy(step, j, buffer, send, recv, to):
+        return pltpu.make_async_remote_copy(
+            src_ref=part.at[step, pl.ds(j * rows, rows)],
+            dst_ref=buffer.at[step, pl.ds(j * rows, rows)],
+            send_sem=send.at[step, j],
+            recv_sem=recv.at[step, j],
+            device_id=(me, to),
+            device_id_type=mesh_ids,
+        )
+
+    def owner(step):
+        there = jnp.where(z < m // 2, spot - step + n, spot + step)
+        return ring_place(lax.rem(there, n), n)
+
+    def out_copy(step, sender):
+        return pltpu.make_async_remote_copy(
+            src_ref=part.at[step, pl.ds(pl.multiple_of(z * rows, rows), rows)],
+            dst_ref=out_ref.at[sender],
+            send_sem=out_send.at[step],
+            recv_sem=out_recv.at[sender],
+            device_id=(owner(step), z),
+            device_id_type=mesh_ids,
+        )
+
+    def added(step, j, buffer):
+        span = pl.ds(j * rows, rows)
+        part[step, span] = (
+            part[step, span].astype(jnp.float32) + buffer[step, span].astype(jnp.float32)
+        ).astype(jnp.bfloat16)
+
+    up_lag, down_lag = z, m - 1 - z
+    last_lag = jnp.maximum(up_lag, down_lag)
+
+    def turn(tau, carry):
+        @pl.when(tau < n)
+        def _():
+            @pl.when(tau > 0)
+            def _():
+                for d in range(2):
+                    gather_arrival(tau, d).wait_recv()
+
+            @pl.when(tau < n - 1)
+            def _():
+                for d in range(2):
+                    gather_copy(tau, d).start()
+
+            block = gat[tau].reshape(2 * half, depth)
+            for c in range(0, width, tile):
+                part[tau, :, c : c + tile] = jnp.dot(
+                    block, w_ref[:, c : c + tile], preferred_element_type=jnp.float32
+                ).astype(jnp.bfloat16)
+
+        t_up = tau - up_lag
+
+        @pl.when((t_up >= 0) & (t_up < n))
+        def _():
+            for j in range(m - 1, 0, -1):
+                @pl.when(z < j)
+                def _():
+                    copy = chain_copy(t_up, j, up, up_send, up_recv, z + 1)
+
+                    @pl.when(z > 0)
+                    def _():
+                        copy.wait_recv()
+                        added(t_up, j, up)
+
+                    copy.start()
+
+        t_down = tau - down_lag
+
+        @pl.when((t_down >= 0) & (t_down < n))
+        def _():
+            for j in range(m - 1):
+                @pl.when(z > j)
+                def _():
+                    copy = chain_copy(t_down, j, down, down_send, down_recv, z - 1)
+
+                    @pl.when(z < m - 1)
+                    def _():
+                        copy.wait_recv()
+                        added(t_down, j, down)
+
+                    copy.start()
+
+        t_last = tau - last_lag
+
+        @pl.when((t_last >= 0) & (t_last < n))
+        def _():
+            for j in range(m):
+                @pl.when(z == j)
+                def _():
+                    span = pl.ds(j * rows, rows)
+                    total = part[t_last, span].astype(jnp.float32)
+                    if j > 0:
+                        chain_copy(t_last, j, up, up_send, up_recv, z).wait_recv()
+                        total = total + up[t_last, span].astype(jnp.float32)
+                    if j < m - 1:
+                        chain_copy(t_last, j, down, down_send, down_recv, z).wait_recv()
+                        total = total + down[t_last, span].astype(jnp.float32)
+                    part[t_last, span] = total.astype(jnp.bfloat16)
+
+            @pl.when(t_last == 0)
+            def _():
+                out_ref[me] = part[0, pl.ds(pl.multiple_of(z * rows, rows), rows)]
+
+            @pl.when(t_last > 0)
+            def _():
+                out_copy(t_last, me).start()
+
+        return carry
+
+    lax.fori_loop(0, n + m - 1, turn, 0)
+
+    def finish(step, carry):
+        @pl.when(step < n - 1)
+        def _():
+            for d in range(2):
+                gather_copy(step, d).wait_send()
+
+        for j in range(m):
+            @pl.when(z < j)
+            def _():
+                chain_copy(step, j, up, up_send, up_recv, z).wait_send()
+
+            @pl.when(z > j)
+            def _():
+                chain_copy(step, j, down, down_send, down_recv, z).wait_send()
+
+        @pl.when(step > 0)
+        def _():
+            out_copy(step, me).wait_send()
+            out_copy(step, lax.rem(me + step, n)).wait_recv()
+
+        return carry
+
+    lax.fori_loop(0, n, finish, 0)
+
+
+def mix(normed, weight):
+    n, m = lax.axis_size("seq"), lax.axis_size("tp")
+    length, depth = normed.shape
+    width = weight.shape[1]
+    rows = length // m
+    half = length // 2
+    slots = pltpu.VMEM((n, length, width), jnp.bfloat16)
+    dma = pltpu.SemaphoreType.DMA
+    vmem = pl.BlockSpec(memory_space=pltpu.VMEM)
+    return pl.pallas_call(
+        functools.partial(mix_kernel, n, m),
+        out_shape=jax.ShapeDtypeStruct((n, rows, width), jnp.bfloat16),
+        in_specs=[pl.BlockSpec(memory_space=pl.ANY), vmem],
+        out_specs=vmem,
+        scratch_shapes=[
+            pltpu.VMEM((n, 2, half, depth), jnp.bfloat16),
+            slots,
+            slots,
+            slots,
+            dma((2,)),
+            dma((n, 2)),
+            dma((n, 2)),
+            dma((n, m)),
+            dma((n, m)),
+            dma((n, m)),
+            dma((n, m)),
+            dma((n,)),
+            dma((n,)),
+        ],
+        compiler_params=pltpu.CompilerParams(
+            collective_id=0, has_side_effects=True, vmem_limit_bytes=48 << 20
+        ),
+        cost_estimate=pl.CostEstimate(
+            flops=2 * n * length * depth * width,
+            bytes_accessed=2 * (depth * width + length * depth),
+            transcendentals=0,
+        ),
+    )(normed, weight)
 
 
 def shards(
@@ -115,13 +372,8 @@
         (gated_out * inv_rms[:, :, None]).reshape(length, heads_dev * HEAD_DIM)
         * norm_weight[None, :]
     ).astype(jnp.bfloat16)
-    weight_full = lax.all_gather(out_weight, "seq", axis=1, tiled=True)
-    summed = lax.psum_scatter(
-        jnp.dot(normed, weight_full, preferred_element_type=jnp.float32).astype(jnp.bfloat16),
-        "tp",
-        scatter_dimension=0,
-        tiled=True,
-    ).astype(jnp.float32)
+    blocks = mix(normed, out_weight)
+    summed = jnp.transpose(blocks, (1, 0, 2)).reshape(residual.shape).astype(jnp.float32)
     return residual.astype(jnp.float32) + summed
 
 

time: 357 us -> 231 us (0.65)
  waiting for transfers between devices: 217 us -> 21.5 us
  Pallas kernels: 0 us -> 84.3 us
  matrix products: 58 us -> 41.1 us
    all_gather x1 -> x0, waiting for transfers between devices: 119 us -> none  [shards(): weight_full = lax.all_gather(out_weight, 'seq', axis=1, tiled=True)]
    pallas_call x0 -> x1, Pallas kernels: none -> 84.3 us  [mix(): pl.pallas_call(functools.partial(mix_kernel, n, m), out_shape=jax.ShapeDt...]
    reduce_scatter x1 -> x0, waiting for transfers between devices: 77 us -> none  [shards(): lax.psum_scatter(jnp.dot(normed, weight_full, preferred_element_type=jnp....]
    dot_general x1 -> x0, matrix products: 16.5 us -> none  [shards(): jnp.dot(normed, weight_full, preferred_element_type=jnp.float32)]
  transfers between devices with their start and end apart: 5 -> 3, of which waited for: 3 -> 1; matrix products, arithmetic and copies ran while one was open for 17% -> 14% of each run, Pallas kernels for 0% -> 0%
where the time goes in v1:
time: 231 us; the launch traced here: 230 us
  Pallas kernels  84.3 us (36%)
  matrix products  41.1 us (18%)
  other arithmetic  23.3 us (10%)
  blocking collectives  22.4 us (10%)
  waiting for transfers between devices  21.5 us (9%)
  local copies, waits for them, and re-layouts  16.5 us (7%)
  between operations  13.8 us (6%)
  starting transfers between devices  6.9 us (3%)
    pallas_call x1, Pallas kernels, mix(): pl.pallas_call(functools.partial(mix_kernel, n, m), out_shape=jax.ShapeDt...  84.3 us
    all_gather x1, waiting for transfers between devices, entering_2(): pieces = jax.tree.map(lambda part: lax.all_gather(part, axis), value)  21.4 us
    dot_general x1, matrix products, shards(): jnp.einsum('thn,shn->hts', output_heads, input_heads, precision=highest)  16.3 us
    all_gather x1, blocking collectives, shards(): all_heads = lax.all_gather(head_squares, 'tp', axis=1, tiled=True)  13.6 us
    select_n x7, other arithmetic, turn(): jnp.where(position < mine, new, old)  10.2 us
    dot_general x1, matrix products, shards(): within = jnp.einsum('hts,shp->thp', mixing, value_heads, precision=highest)  9.09 us
    all_gather x1, blocking collectives, entering_2(): pieces = jax.tree.map(lambda part: lax.all_gather(part, axis), value)  8.79 us
    unnamed x27, local copies, waits for them, and re-layouts  8.15 us
  transfers between devices with their start and end apart: 3, of which 1 were waited for; matrix products, arithmetic and copies ran while one was open for 14% of the time, Pallas kernels for 0%

profile of v1, /device:TPU:0, one launch (start us, length us, event | category | flops | bytes accessed | tf_op | source)
XLA Modules:
  0.0 229.9 jit_solution(17125543382914141490)
XLA Ops:
  6.5 0.9 slice.75
  7.4 2.4 %collective-permute-start.1 = (bf16[3,2048]{1,0:T(4,128)(2,1)S(1)}, bf16[3,2048]{1,0:T(4,128)(2,1)S(1)}, u32[]{:S(2)}, u32[]{:S(2)}) collective-permute-start(bf16[3,2048]{1,0:T(4,128)(2,1)S(1)} %slice.75), channel_id=1, source_target_pairs={{0,4},{4,8},{8,12},{12,16},{16,20},{20,24},{24,28},{1,5},{5,9},{9,... | collective-permute-start | bytes 36872 | tf_op jit(solution)/shard_map/ppermute | solution.py:20
  9.8 0.8 slice.65
  10.6 4.5 %collective-permute-start = (bf16[3,2048]{1,0:T(4,128)(2,1)S(1)}, bf16[3,2048]{1,0:T(4,128)(2,1)S(1)}, u32[]{:S(2)}, u32[]{:S(2)}) collective-permute-start(bf16[3,2048]{1,0:T(4,128)(2,1)S(1)} %slice.65), channel_id=1, source_target_pairs={{0,4},{4,8},{8,12},{12,16},{16,20},{20,24},{24,28},{1,5},{5,9},{9,... | collective-permute-start | bytes 36872 | tf_op jit(solution)/shard_map/ppermute | solution.py:20
  15.1 0.9 fusion.58
  16.0 0.7 exponential_negate_fusion
  16.7 0.8 copy_bitcast_fusion.1
  17.5 0.6 reduce-window.6
  18.6 0.9 bitcast_exponential_fusion
  19.4 0.9 fusion.59
  20.4 1.5 convert_element_type.45
  21.9 0.2 convert_element_type.42
  22.2 0.4 copy-done.8
  22.6 1.4 multiply_convert_fusion.1
  24.0 0.9 slice_bitcast_fusion.1
  25.0 1.4 multiply_convert_fusion.2
  26.4 0.5 copy.28
  27.0 0.7 convolution_bitcast_fusion
  27.7 0.2 copy-done.3
  28.0 1.7 copy-done.1
  29.7 6.1 %fusion.13 = f32[32,64,128]{2,1,0:T(8,128)} fusion(f32[256,32,128]{2,1,0:T(8,128)S(1)} %convolution_bitcast_fusion, bf16[256,32,64]{0,2,1:T(8,128)(2,1)S(1)} %bitcast.83, f32[256,32]{0,1:T(8,128)S(1)} %get-tuple-element.133), kind=kOutput, calls=%fused_computation.15 | convolution fusion | flops 806354944 | bytes 6324224 | tf_op jit(solution)/shard_map/shp,shn->hpn/dot_general | solution.py:345
  35.8 1.8 convert_multiply_fusion
  37.6 1.8 copy.35
  39.4 8.8 %all-gather.1 = f32[8,1,32]{2,1,0:T(1,128)S(1)} all-gather(f32[1,1,32]{2,1,0:T(1,128)S(1)} %bitcast.98), channel_id=1, replica_groups=mesh['seq'=8,'tp'=4] {'seq'}, dimensions={0}, use_global_device_ids=true | all-gather | bytes 1152 | tf_op jit(solution)/shard_map/all_gather | solution.py:25
  48.2 1.1 copy.41
  49.4 0.7 convolution_bitcast_fusion.1
  50.1 2.0 copy-done
  52.1 0.7 copy-done.2
  52.8 16.3 %fusion.15 = f32[32,256,256]{2,1,0:T(8,128)} fusion(f32[256,32,128]{2,1,0:T(8,128)S(1)} %copy-done.2, f32[256,32,128]{2,1,0:T(8,128)S(1)} %convolution_bitcast_fusion.1), kind=kOutput, calls=%fused_computation.17 | convolution fusion | flops 3221225472 | bytes 16777216 | tf_op jit(solution)/shard_map/thn,shn->hts/dot_general | solution.py:341
  69.1 21.4 %all-gather.4.cloned.1.call-done = f32[256,64,128]{2,1,0:T(8,128)} async-done(((f32[32,64,128]{2,1,0:T(8,128)}), f32[256,64,128]{2,1,0:T(8,128)}) %all-gather.4.cloned.1.call-update) | async-done | bytes 8388624 | tf_op jit(solution)/shard_map/all_gather | solution.py:25
  90.5 10.5 %while.14 = (s32[]{:T(128)}, f32[32,64,128]{2,1,0:T(8,128)S(1)}, s32[]{:T(128)}, f32[8,32]{1,0:T(8,128)S(1)}, f32[8,32,64,128]{3,2,1,0:T(8,128)}, /*index=5*/s32[]{:T(128)}, s32[]{:T(128)}) while((s32[]{:T(128)}, f32[32,64,128]{2,1,0:T(8,128)S(1)}, s32[]{:T(128)}, f32[8,32]{1,0:T(8,128)S(1)}, f32[8,32,64,128]{3,2,1,0:T(8,128)}, ...), condition=%wide.region_3.4_spmd.clone, body=%wide.region_2.3_spmd.clone.sunk | while | flops 1048580 | bytes 3146217 | solution.py:34
  90.5 1.5 fusion.66
  92.0 1.5 fusion.66
  93.5 1.5 fusion.66
  95.0 1.5 fusion.66
  96.5 1.5 fusion.66
  98.0 1.5 fusion.66
  99.5 1.5 fusion.66
  101.0 8.0 %fusion.17 = f32[32,64,256]{2,1,0:T(8,128)S(1)} fusion(f32[32,64,128]{2,1,0:T(8,128)S(1)} %get-tuple-element.99, f32[256,32,128]{2,1,0:T(8,128)} %copy-done), kind=kOutput, calls=%fused_computation.19 | convolution fusion | flops 805306368 | bytes 7340032 | tf_op jit(solution)/shard_map/thn,hpn->thp/dot_general | solution.py:359
  109.0 9.1 %multiply_reduce_fusion = (f32[256,32]{0,1:T(8,128)S(1)}, f32[256,32,64]{0,2,1:T(8,128)S(1)}) fusion(f32[256,32,64]{0,2,1:T(8,128)S(1)} %bitcast.88, bf16[256,32,64]{0,2,1:T(8,128)(2,1)S(1)} %bitcast.84, f32[32]{0:T(128)S(1)} %copy-done.11, f32[256,32]{0,1:T(8,128)S(1)} %get-tuple-element.132, f32[32,64,256]{2,1,0:T(8,128)S(1)} %fusion.17, ...), kind=kOutput, calls=%fused_computation.61 | convolution fusion | flops 1625284608 | bytes 15925376 | tf_op jit(solution)/shard_map/hts,shp->thp/dot_general | solution.py:343
  118.1 13.6 %all_gather.16 = f32[256,128]{0,1:T(8,128)S(1)} all-gather(f32[256,32]{0,1:T(8,128)S(1)} %get-tuple-element.145), channel_id=1, replica_groups=mesh['seq'=8,'tp'=4] {'tp'}, dimensions={1}, use_global_device_ids=true | all-gather | bytes 163840 | tf_op jit(solution)/shard_map/all_gather | solution.py:367
  132.2 1.8 copy.36
  134.0 1.8 multiply_convert_fusion.x_ref
  135.8 84.3 %shard_map.127 = bf16[8,64,1024]{2,1,0:T(8,128)(2,1)S(1)} custom-call(bf16[256,2048]{1,0:T(8,128)(2,1)S(1)} %multiply_convert_fusion.x_ref, bf16[2048,1024]{1,0:T(8,128)(2,1)} %w_ref.1), custom_call_target="tpu_custom_call" | custom-call | flops 8589934592 | bytes 5242880 | tf_op jit(solution)/shard_map/pallas_call | solution.py:268
  220.1 0.2 convert_bitcast_fusion
  220.3 0.2 copy.40
  220.6 1.0 copy-done.7
  221.5 1.5 convert_add_fusion
  (43 shorter events, 1.2 us)
Async XLA Ops:
  6.5 15.3 %copy-start.6 = (bf16[256,2048]{1,0:T(8,128)(2,1)S(1)}, bf16[256,2048]{1,0:T(8,128)(2,1)}, u32[]{:S(2)}) copy-start(bf16[256,2048]{1,0:T(8,128)(2,1)} %param.15) | copy-start | bytes 3145732
  6.5 84.0 %all-gather.4.cloned.1.call-start = ((), (), s32[]{:S(2)}) async-start(), calls=%async_computation | async-start | bytes 9437184 | tf_op jit(solution)/shard_map/all_gather | solution.py:25
  7.4 14.7 %collective-permute-start.1 = (bf16[3,2048]{1,0:T(4,128)(2,1)S(1)}, bf16[3,2048]{1,0:T(4,128)(2,1)S(1)}, u32[]{:S(2)}, u32[]{:S(2)}) collective-permute-start(bf16[3,2048]{1,0:T(4,128)(2,1)S(1)} %slice.75), channel_id=1, source_target_pairs={{0,4},{4,8},{8,12},{12,16},{16,20},{20,24},{24,28},{1,5},{5,9},{9,... | collective-permute-start | bytes 36872 | tf_op jit(solution)/shard_map/ppermute | solution.py:20
  10.6 14.4 %collective-permute-start = (bf16[3,2048]{1,0:T(4,128)(2,1)S(1)}, bf16[3,2048]{1,0:T(4,128)(2,1)S(1)}, u32[]{:S(2)}, u32[]{:S(2)}) collective-permute-start(bf16[3,2048]{1,0:T(4,128)(2,1)S(1)} %slice.65), channel_id=1, source_target_pairs={{0,4},{4,8},{8,12},{12,16},{16,20},{20,24},{24,28},{1,5},{5,9},{9,... | collective-permute-start | bytes 36872 | tf_op jit(solution)/shard_map/ppermute | solution.py:20
  21.9 0.7 copy-start.8
  24.0 1.0 copy-start.9
  27.0 1.0 copy-start.3
  27.7 1.9 copy-start.1
  49.3 3.4 %copy-start.2 = (f32[256,32,128]{2,1,0:T(8,128)S(1)}, f32[256,32,128]{2,1,0:T(8,128)}, u32[]{:S(2)}) copy-start(f32[256,32,128]{2,1,0:T(8,128)} %copy-done.1) | copy-start | bytes 12582916
  50.1 2.0 copy-start
  101.0 8.0 %copy-start.4 = (bf16[256,2048]{0,1:T(8,128)(2,1)S(1)}, bf16[256,2048]{0,1:T(8,128)(2,1)}, u32[]{:S(2)}) copy-start(bf16[256,2048]{0,1:T(8,128)(2,1)} %copy-done.3) | copy-start | bytes 3145732
  101.0 8.0 %copy-start.5 = (f32[256,2048]{0,1:T(8,128)S(1)}, f32[256,2048]{0,1:T(8,128)}, u32[]{:S(2)}) copy-start(f32[256,2048]{0,1:T(8,128)} %copy.35) | copy-start | bytes 6291460
  101.0 8.0 %copy-start.11 = (f32[32]{0:T(128)S(1)}, f32[32]{0:T(128)}, u32[]{:S(2)}) copy-start(f32[32]{0:T(128)} %param.20) | copy-start | bytes 388
  132.2 1.8 copy-start.10
  220.3 1.2 copy-start.7
Sparse Core Ops, SparseCore 0:
  35.9 54.5 all-gather.3

commit v2 on v1

--- a/solution.py
+++ b/solution.py
@@ -12,35 +12,6 @@
 STATE = 128
 GROUPS = 8
 CONV = 4
-
-
-def passed_along(array, axis, by):
-    size = lax.axis_size(axis)
-    pairs = [(i, i + by) for i in range(size) if 0 <= i + by < size]
-    return lax.ppermute(array, axis, pairs)
-
-
-def entering_2(value, axis, join, neutral):
-    count, mine = (lax.axis_size(axis), lax.axis_index(axis))
-    pieces = jax.tree.map(lambda part: lax.all_gather(part, axis), value)
-    subtotal = jax.tree.map(
-        lambda part, zero: jnp.full_like(part, 0) + jnp.asarray(zero, part.dtype), value, neutral
-    )
-
-    def turn(position, subtotal):
-        longer = join(subtotal, jax.tree.map(lambda part: part[position], pieces))
-        return jax.tree.map(lambda new, old: jnp.where(position < mine, new, old), longer, subtotal)
-
-    return lax.fori_loop(0, count - 1, turn, subtotal)
-
-
-def rim_conv(rim_rows, local_rows, kernel, offset):
-    length = local_rows.shape[0]
-    padded = jnp.concatenate([rim_rows.astype(jnp.float32), local_rows.astype(jnp.float32)], axis=0)
-    summed = offset[None, :] + kernel[0][None, :] * padded[0:length]
-    for position in range(1, CONV):
-        summed = summed + kernel[position][None, :] * padded[position : position + length]
-    return jax.nn.silu(summed).astype(jnp.bfloat16)
 
 
 def ring_place(spot, size):
@@ -296,6 +267,263 @@
     )(normed, weight)
 
 
+def front_kernel(
+    n, per_group, whole_groups, x_ref, gate_ref, maps_ref, cum_ref, cum_t_ref, step_ref, step_t_ref,
+    decay_ref, skip_ref, taps_ref, base_ref, map_taps_ref, map_base_ref, gain_ref, out_ref,
+    rim_x, rim_maps, pad, values, y, b_maps, c_maps, scores, local, arrived, leaving,
+    rim_send, rim_recv, chain_send, chain_recv,
+):
+    mesh_ids = pl.DeviceIdType.MESH
+    exact = lax.Precision.HIGHEST
+    me, z = lax.axis_index("seq"), lax.axis_index("tp")
+    length, channels = x_ref.shape
+    heads = cum_ref.shape[1]
+    groups_here = scores.shape[0]
+    first_group = lax.div(z * heads, per_group)
+    tile = arrived.shape[2]
+    tiles = channels // tile
+    group_width = channels // groups_here
+    rim = rim_x.shape[0]
+
+    barrier = pltpu.get_barrier_semaphore()
+    has_left, has_right = me > 0, me < n - 1
+
+    @pl.when(has_left)
+    def _():
+        pl.semaphore_signal(barrier, inc=1, device_id=(me - 1, z), device_id_type=mesh_ids)
+
+    @pl.when(has_right)
+    def _():
+        pl.semaphore_signal(barrier, inc=1, device_id=(me + 1, z), device_id_type=mesh_ids)
+
+    pl.semaphore_wait(barrier, has_left.astype(jnp.int32) + has_right.astype(jnp.int32))
+
+    def rim_copy(which):
+        source, target = ((x_ref, rim_x), (maps_ref, rim_maps))[which]
+        return pltpu.make_async_remote_copy(
+            src_ref=source.at[pl.ds(length - rim, rim)],
+            dst_ref=target,
+            send_sem=rim_send.at[which],
+            recv_sem=rim_recv.at[which],
+            device_id=(me + 1, z),
+            device_id_type=mesh_ids,
+        )
+
+    @pl.when(has_right)
+    def _():
+        for which in range(2):
+            rim_copy(which).start()
+
+    @pl.when(has_left)
+    def _():
+        for which in range(2):
+            rim_copy(which).wait_recv()
+
+    @pl.when(jnp.logical_not(has_left))
+    def _():
+        rim_x[...] = jnp.zeros_like(rim_x)
+        rim_maps[...] = jnp.zeros_like(rim_maps)
+
+    def conv(rows_ref, rim_ref, taps, base, start, size):
+        span = pl.ds(start, size)
+        pad[0:rim, 0:size] = rim_ref[:, span].astype(jnp.float32)
+        pad[rim : rim + length, 0:size] = rows_ref[:, span].astype(jnp.float32)
+        total = base[:, span]
+        for k in range(CONV):
+            at = rim - (CONV - 1) + k
+            total = total + taps[k : k + 1, span] * pad[at : at + length, 0:size]
+        return jax.nn.silu(total).astype(jnp.bfloat16)
+
+    for g in range(groups_here):
+        at = pl.multiple_of((first_group + g) * STATE, STATE)
+        b_maps[g] = conv(maps_ref, rim_maps, map_taps_ref, map_base_ref, at, STATE)
+        at = pl.multiple_of((GROUPS + first_group + g) * STATE, STATE)
+        c_maps[g] = conv(maps_ref, rim_maps, map_taps_ref, map_base_ref, at, STATE)
+        scores[g] = lax.dot_general(
+            c_maps[g], b_maps[g], (((1,), (1,)), ((), ())), preferred_element_type=jnp.float32
+        )
+
+    def spread(per_head, start):
+        head = lax.broadcasted_iota(jnp.int32, (heads, tile), 0) * HEAD_DIM
+        lane = lax.broadcasted_iota(jnp.int32, (heads, tile), 1) + start
+        chosen = ((lane >= head) & (lane < head + HEAD_DIM)).astype(jnp.float32)
+        return jnp.dot(
+            per_head, chosen, precision=exact, preferred_element_type=jnp.float32
+        )
+
+    cum = cum_ref[...]
+    end_weight = jnp.exp(cum[length - 1 : length] - cum) * step_ref[...]
+    grown = jnp.exp(cum)
+
+    def states(c, carry):
+        start = pl.multiple_of(c * tile, tile)
+        span = pl.ds(start, tile)
+        value = conv(x_ref, rim_x, taps_ref, base_ref, start, tile)
+        values[:, span] = value
+        weighted = (value.astype(jnp.float32) * spread(end_weight, start)).astype(jnp.bfloat16)
+        g = lax.div(start, group_width)
+        local[c] = lax.dot_general(
+            b_maps[g], weighted, (((0,), (0,)), ((), ())), preferred_element_type=jnp.float32
+        )
+        return carry
+
+    lax.fori_loop(0, tiles, states, 0)
+
+    def chain_copy(c):
+        return pltpu.make_async_remote_copy(
+            src_ref=leaving.at[c],
+            dst_ref=arrived.at[c],
+            send_sem=chain_send.at[c],
+            recv_sem=chain_recv.at[c],
+            device_id=(me + 1, z),
+            device_id_type=mesh_ids,
+        )
+
+    def link(c, carry):
+        span = pl.ds(pl.multiple_of(c * tile, tile), tile)
+
+        @pl.when(has_left)
+        def _():
+            chain_copy(c).wait_recv()
+
+        @pl.when(jnp.logical_not(has_left))
+        def _():
+            arrived[c] = jnp.zeros_like(arrived[c])
+
+        @pl.when(has_right)
+        def _():
+            leaving[c] = (
+                decay_ref[:, span] * arrived[c].astype(jnp.float32) + local[c]
+            ).astype(jnp.bfloat16)
+            chain_copy(c).start()
+
+        return carry
+
+    pair = 2 * HEAD_DIM
+    causal = lax.broadcasted_iota(jnp.int32, (length, length), 0) >= lax.broadcasted_iota(
+        jnp.int32, (length, length), 1
+    )
+
+    def within(q, carry):
+        span = pl.ds(pl.multiple_of(q * pair, pair), pair)
+        value = values[:, span]
+        g = lax.div(q * pair, group_width)
+        sums = []
+        for e in range(2):
+            h = 2 * q + e
+            lane = lax.broadcasted_iota(jnp.int32, (length, heads), 1)
+            column = jnp.sum(jnp.where(lane == h, cum_ref[...], 0.0), axis=1, keepdims=True)
+            gap = column - cum_t_ref[pl.ds(h, 1), :]
+            kernel = jnp.where(causal, jnp.exp(jnp.where(causal, gap, 0.0)), 0.0)
+            mixing = kernel * scores[g] * step_t_ref[pl.ds(h, 1), :]
+            sums.append(
+                jnp.dot(mixing.astype(jnp.bfloat16), value, preferred_element_type=jnp.float32)
+            )
+        first = lax.broadcasted_iota(jnp.int32, (length, pair), 1) < HEAD_DIM
+        y[:, span] = jnp.where(first, sums[0], sums[1])
+        return carry
+
+    late = me >= n // 2
+
+    def phase(turn, carry):
+        @pl.when((turn == 0) == late)
+        def _():
+            lax.fori_loop(0, channels // pair, within, 0)
+
+        @pl.when(turn == 0)
+        def _():
+            lax.fori_loop(0, tiles, link, 0)
+
+        return carry
+
+    lax.fori_loop(0, 2, phase, 0)
+
+    for g in range(groups_here):
+        per = group_width // tile
+
+        def gated(c, squares):
+            c = c + g * per
+            start = pl.multiple_of(c * tile, tile)
+            span = pl.ds(start, tile)
+            carried = jnp.dot(
+                c_maps[g], arrived[c], preferred_element_type=jnp.float32
+            ) * spread(grown, start)
+            total = y[:, span] + carried + skip_ref[:, span] * values[:, span].astype(jnp.float32)
+            total = total * jax.nn.silu(gate_ref[:, span].astype(jnp.float32))
+            y[:, span] = total
+            return squares + jnp.sum(total * total, axis=1, keepdims=True)
+
+        squares = lax.fori_loop(0, per, gated, jnp.zeros((length, 1), jnp.float32))
+        scale = lax.rsqrt(squares / group_width + 1e-05)
+
+        def scaled(c, carry):
+            span = pl.ds(pl.multiple_of((c + g * per) * tile, tile), tile)
+            if whole_groups:
+                out_ref[:, span] = (y[:, span] * scale * gain_ref[:, span]).astype(out_ref.dtype)
+            else:
+                out_ref[:, span] = y[:, span]
+            return carry
+
+        lax.fori_loop(0, per, scaled, 0)
+
+    @pl.when(has_right)
+    def _():
+        for which in range(2):
+            rim_copy(which).wait_send()
+
+        def sent(c, carry):
+            chain_copy(c).wait_send()
+            return carry
+
+        lax.fori_loop(0, tiles, sent, 0)
+
+
+def front(x, gate, maps, cum, step, skip, taps, base, map_taps, map_base, gain, whole_groups):
+    n = lax.axis_size("seq")
+    length, channels = x.shape
+    heads = cum.shape[1]
+    per_group = HEADS // GROUPS
+    groups_here = max(1, heads // per_group)
+    tile = max(128, channels // 8)
+    tiles = channels // tile
+    rim = 16
+    bf16, f32 = jnp.bfloat16, jnp.float32
+    dma = pltpu.SemaphoreType.DMA
+    vmem = pl.BlockSpec(memory_space=pltpu.VMEM)
+    decay = jnp.repeat(jnp.exp(cum[-1]), HEAD_DIM)[None]
+    skips = jnp.repeat(skip, HEAD_DIM)[None]
+    operands = (
+        x, gate, maps, cum, cum.T, step, step.T, decay, skips,
+        taps, base[None], map_taps, map_base[None], gain[None],
+    )
+    return pl.pallas_call(
+        functools.partial(front_kernel, n, per_group, whole_groups),
+        out_shape=jax.ShapeDtypeStruct((length, channels), bf16 if whole_groups else f32),
+        in_specs=[vmem] * len(operands),
+        out_specs=vmem,
+        scratch_shapes=[
+            pltpu.VMEM((rim, channels), bf16),
+            pltpu.VMEM((rim, maps.shape[1]), bf16),
+            pltpu.VMEM((rim + length, max(tile, STATE)), f32),
+            pltpu.VMEM((length, channels), bf16),
+            pltpu.VMEM((length, channels), f32),
+            pltpu.VMEM((groups_here, length, STATE), bf16),
+            pltpu.VMEM((groups_here, length, STATE), bf16),
+            pltpu.VMEM((groups_here, length, length), f32),
+            pltpu.VMEM((tiles, STATE, tile), f32),
+            pltpu.VMEM((tiles, STATE, tile), bf16),
+            pltpu.VMEM((tiles, STATE, tile), bf16),
+            dma((2,)),
+            dma((2,)),
+            dma((tiles,)),
+            dma((tiles,)),
+        ],
+        compiler_params=pltpu.CompilerParams(
+            collective_id=1, has_side_effects=True, vmem_limit_bytes=48 << 20
+        ),
+    )(*operands)
+
+
 def shards(
     conv_values,
     gate_values,
@@ -311,67 +539,29 @@
     out_weight,
     residual,
 ):
-    highest = lax.Precision.HIGHEST
     length = conv_values.shape[0]
     heads_dev = decay_log.shape[0]
-    rim_count = CONV - 1
-    rim_inner, rim_maps = passed_along(
-        (conv_values[length - rim_count :], conv_maps[length - rim_count :]), "seq", 1
+    per_group = HEADS // GROUPS
+    whole_groups = heads_dev % per_group == 0
+    step_size = jax.nn.softplus(step_raw)
+    cum_log = jnp.cumsum(-jnp.exp(decay_log)[None, :] * step_size, axis=0)
+    normed = front(
+        conv_values, gate_values, conv_maps, cum_log, step_size, skip_gain, values_kernel,
+        values_offset, maps_kernel, maps_offset, norm_weight, whole_groups,
     )
-    values_conv = rim_conv(rim_inner, conv_values, values_kernel, values_offset)
-    maps_conv = rim_conv(rim_maps, conv_maps, maps_kernel, maps_offset)
-    step_size = jax.nn.softplus(step_raw)
-    log_decay = -jnp.exp(decay_log)[None, :] * step_size
-    cum_log = jnp.cumsum(log_decay, axis=0)
-    heads_here = lax.axis_index("tp") * heads_dev + jnp.arange(heads_dev, dtype=jnp.int32)
-    group_of = heads_here * GROUPS // HEADS
-    one_hot = (group_of[:, None] == jnp.arange(GROUPS, dtype=jnp.int32)[None, :]).astype(
-        jnp.float32
-    )
-    input_groups = maps_conv[:, : GROUPS * STATE].astype(jnp.float32).reshape(length, GROUPS, STATE)
-    output_groups = (
-        maps_conv[:, GROUPS * STATE :].astype(jnp.float32).reshape(length, GROUPS, STATE)
-    )
-    input_heads = jnp.einsum("hg,qgn->qhn", one_hot, input_groups, precision=highest)
-    output_heads = jnp.einsum("hg,qgn->qhn", one_hot, output_groups, precision=highest)
-    value_heads = values_conv.astype(jnp.float32).reshape(length, heads_dev, HEAD_DIM)
-    causal = jnp.tril(jnp.ones((length, length), dtype=bool))
-    gap_log = cum_log.T[:, :, None] - cum_log.T[:, None, :]
-    kernel = jnp.where(causal[None], jnp.exp(jnp.where(causal[None], gap_log, 0.0)), 0.0)
-    scores = jnp.einsum("thn,shn->hts", output_heads, input_heads, precision=highest)
-    mixing = kernel * scores * step_size.T[:, None, :]
-    within = jnp.einsum("hts,shp->thp", mixing, value_heads, precision=highest)
-    end_weight = jnp.exp(cum_log[-1][None, :] - cum_log) * step_size
-    local_state = jnp.einsum(
-        "shp,shn->hpn", value_heads * end_weight[:, :, None], input_heads, precision=highest
-    )
-    shard_decay = jnp.exp(cum_log[-1])
-    zeros_state = jnp.zeros_like(local_state)
-
-    def combine(earlier, latter):
-        return (earlier[0] * latter[0], latter[0][:, None, None] * earlier[1] + latter[1])
-
-    prefix = entering_2(
-        (shard_decay, local_state), "seq", combine, (jnp.ones_like(shard_decay), zeros_state)
-    )
-    entering = prefix[1]
-    carried = (
-        jnp.einsum("thn,hpn->thp", output_heads, entering, precision=highest)
-        * jnp.exp(cum_log)[:, :, None]
-    )
-    mixer_out = within + carried + skip_gain[None, :, None] * value_heads
-    gated_out = mixer_out * jax.nn.silu(gate_values.astype(jnp.float32)).reshape(
-        length, heads_dev, HEAD_DIM
-    )
-    head_squares = jnp.sum(gated_out * gated_out, axis=2)
-    all_heads = lax.all_gather(head_squares, "tp", axis=1, tiled=True)
-    group_totals = jnp.sum(all_heads.reshape(length, GROUPS, HEADS // GROUPS), axis=2)
-    group_squares = jnp.einsum("qg,hg->qh", group_totals, one_hot, precision=highest)
-    inv_rms = lax.rsqrt(group_squares / (HEADS // GROUPS * HEAD_DIM) + 1e-05)
-    normed = (
-        (gated_out * inv_rms[:, :, None]).reshape(length, heads_dev * HEAD_DIM)
-        * norm_weight[None, :]
-    ).astype(jnp.bfloat16)
+    if not whole_groups:
+        gated_out = normed.reshape(length, heads_dev, HEAD_DIM)
+        head_squares = jnp.sum(gated_out * gated_out, axis=2)
+        all_heads = lax.all_gather(head_squares, "tp", axis=1, tiled=True)
+        group_totals = jnp.sum(all_heads.reshape(length, GROUPS, per_group), axis=2)
+        heads_here = lax.axis_index("tp") * heads_dev + jnp.arange(heads_dev, dtype=jnp.int32)
+        inv_rms = lax.rsqrt(
+            group_totals[:, heads_here // per_group] / (per_group * HEAD_DIM) + 1e-05
+        )
+        normed = (
+            (gated_out * inv_rms[:, :, None]).reshape(length, heads_dev * HEAD_DIM)
+            * norm_weight[None, :]
+        ).astype(jnp.bfloat16)
     blocks = mix(normed, out_weight)
     summed = jnp.transpose(blocks, (1, 0, 2)).reshape(residual.shape).astype(jnp.float32)
     return residual.astype(jnp.float32) + summed

time: 231 us -> 130 us (0.56)
  matrix products: 41.1 us -> 0 us
  Pallas kernels: 84.3 us -> 115 us
  blocking collectives: 22.4 us -> 0 us
  waiting for transfers between devices: 21.5 us -> 0 us
  other arithmetic: 23.3 us -> 3.92 us
  between operations: 13.8 us -> 0.07 us
  starting transfers between devices: 6.9 us -> 0 us
  local copies, waits for them, and re-layouts: 16.5 us -> 10 us
    dot_general x7 -> x0, matrix products: 41.1 us -> none  [the longest x1 16.3 us: shards(): jnp.einsum('thn,shn->hts', output_heads, input_heads, precision=highest)]
    all_gather x2 -> x0, blocking collectives: 22.4 us -> none  [the longest x1 13.6 us: shards(): all_heads = lax.all_gather(head_squares, 'tp', axis=1, tiled=True)]
    all_gather x1 -> x0, waiting for transfers between devices: 21.4 us -> none  [entering_2(): pieces = jax.tree.map(lambda part: lax.all_gather(part, axis), value)]
    pallas_call x0 -> x1, Pallas kernels: none -> 16.4 us  [front(): pl.pallas_call(functools.partial(front_kernel, n, per_group, whole_groups...]
    pallas_call x1, Pallas kernels: 84.3 us -> 98.9 us  [mix(): pl.pallas_call(functools.partial(mix_kernel, n, m), out_shape=jax.ShapeDt...]
    select_n x8 -> x0, other arithmetic: 10.2 us -> none  [the longest x7 10.2 us: turn(): jnp.where(position < mine, new, old)]
    ppermute x2 -> x0, starting transfers between devices: 6.9 us -> none  [passed_along(): return lax.ppermute(array, axis, pairs)]
    convert_element_type x7 -> x0, other arithmetic: 6.26 us -> none  [the longest x2 2.8 us: rim_conv(): return jax.nn.silu(summed).astype(jnp.bfloat16)]
  transfers between devices with their start and end apart: 3 -> 0, of which waited for: 1 -> 0; matrix products, arithmetic and copies ran while one was open for 14% -> 0% of each run, Pallas kernels for 0% -> 0%
where the time goes in v2:
time: 130 us; the launch traced here: 129 us
  Pallas kernels  115 us (88%)
  local copies, waits for them, and re-layouts  10 us (8%)
  other arithmetic  3.92 us (3%)
    pallas_call x1, Pallas kernels, mix(): pl.pallas_call(functools.partial(mix_kernel, n, m), out_shape=jax.ShapeDt...  98.9 us
    pallas_call x1, Pallas kernels, front(): pl.pallas_call(functools.partial(front_kernel, n, per_group, whole_groups...  16.4 us
    unnamed x18, local copies, waits for them, and re-layouts  8.25 us

profile of v2, /device:TPU:0, one launch (start us, length us, event | category | flops | bytes accessed | tf_op | source)
XLA Modules:
  0.0 129.3 jit_solution(15126026654219764029)
XLA Ops:
  0.0 0.7 exponential_negate_fusion
  0.7 0.7 broadcast_in_dim.17
  1.4 0.1 broadcast_in_dim_reshape.7.skip_ref
  1.5 0.8 fusion.2
  2.3 0.6 reduce-window.6
  2.9 0.2 slice_reduce_fusion
  3.1 0.1 copy_bitcast_fusion
  3.2 0.2 fusion
  3.4 0.1 broadcast_in_dim.16
  3.4 0.1 broadcast_in_dim_reshape.6.decay_ref
  3.5 0.1 copy.20.cum_ref
  3.6 0.1 copy.21.step_ref
  3.7 0.0 copy-start
  3.7 1.2 copy-done
  5.0 0.0 copy-start.1
  5.0 1.2 copy-done.1
  6.2 0.0 copy-start.2
  6.2 1.2 copy-done.2
  7.4 0.0 copy-start.3
  7.4 0.8 copy-done.3
  8.2 0.0 copy-start.4
  8.2 0.8 copy-done.4
  8.9 0.0 copy-start.5
  8.9 0.7 copy-done.5
  9.6 0.0 copy-start.6
  9.6 0.7 copy-done.6
  10.3 0.0 copy-start.7
  10.3 0.7 copy-done.7
  11.0 16.4 %shard_map.127.x_ref = bf16[256,2048]{1,0:T(8,128)(2,1)S(1)} custom-call(bf16[256,2048]{1,0:T(8,128)(2,1)S(1)} %copy-done, bf16[256,2048]{1,0:T(8,128)(2,1)S(1)} %copy-done.1, bf16[256,2048]{1,0:T(8,128)(2,1)S(1)} %copy-done.2, f32[256,32]{1,0:T(8,128)S(1)} %copy.20.cum_ref, f32[32,256]{1,0:T(8,128)S(1)} %get-tuple-element.8.cum_t_ref, ...), custom_call_target="tpu_custom_call" | custom-call | tf_op jit(solution)/shard_map/pallas_call | solution.py:499
  27.4 98.9 %shard_map.128 = bf16[8,64,1024]{2,1,0:T(8,128)(2,1)S(1)} custom-call(bf16[256,2048]{1,0:T(8,128)(2,1)S(1)} %shard_map.127.x_ref, bf16[2048,1024]{1,0:T(8,128)(2,1)} %w_ref.1), custom_call_target="tpu_custom_call" | custom-call | flops 8589934592 | bytes 5242880 | tf_op jit(solution)/shard_map/pallas_call | solution.py:239
  126.3 0.2 convert_bitcast_fusion
  126.6 0.0 copy-start.8
  126.6 0.2 copy.25
  126.8 1.0 copy-done.8
  127.8 1.5 %convert_add_fusion = f32[64,8192]{1,0:T(8,128)} fusion(f32[64,8192]{1,0:T(8,128)S(1)} %bitcast.27, bf16[64,8192]{1,0:T(8,128)(2,1)S(1)} %copy-done.8), kind=kLoop, calls=%fused_computation.1 | loop fusion | flops 1048576 | bytes 5242880 | tf_op jit(solution)/shard_map/add | solution.py:567
  (3 shorter events, 0.0 us)
Async XLA Ops:
  3.7 1.2 copy-start
  5.0 1.2 copy-start.1
  6.2 1.2 copy-start.2
  7.4 0.8 copy-start.3
  8.2 0.8 copy-start.4
  8.9 0.7 copy-start.5
  9.6 0.7 copy-start.6
  10.3 0.7 copy-start.7
  126.6 1.2 copy-start.8

commit v3 on v2

--- a/solution.py
+++ b/solution.py
@@ -268,9 +268,10 @@
 
 
 def front_kernel(
-    n, per_group, whole_groups, x_ref, gate_ref, maps_ref, cum_ref, cum_t_ref, step_ref, step_t_ref,
-    decay_ref, skip_ref, taps_ref, base_ref, map_taps_ref, map_base_ref, gain_ref, out_ref,
-    rim_x, rim_maps, pad, values, y, b_maps, c_maps, scores, local, arrived, leaving,
+    n, per_group, whole_groups, x_hbm, gate_hbm, maps_hbm, taps_hbm, base_hbm, map_taps_hbm,
+    map_base_hbm, gain_hbm, cum_ref, cum_t_ref, step_ref, step_t_ref, decay_ref, skip_ref, out_ref,
+    x_ref, gate_ref, maps_ref, taps_ref, base_ref, map_taps_ref, map_base_ref, gain_ref,
+    load_sem, rim_x, rim_maps, pad, values, y, b_maps, c_maps, scores, local, arrived, leaving,
     rim_send, rim_recv, chain_send, chain_recv,
 ):
     mesh_ids = pl.DeviceIdType.MESH
@@ -285,6 +286,24 @@
     group_width = channels // groups_here
     rim = rim_x.shape[0]
 
+    loads = [
+        pltpu.make_async_copy(source, target, load_sem.at[i])
+        for i, (source, target) in enumerate(
+            (
+                (maps_hbm, maps_ref),
+                (map_taps_hbm, map_taps_ref),
+                (map_base_hbm, map_base_ref),
+                (x_hbm, x_ref),
+                (taps_hbm, taps_ref),
+                (base_hbm, base_ref),
+                (gate_hbm, gate_ref),
+                (gain_hbm, gain_ref),
+            )
+        )
+    ]
+    for load in loads:
+        load.start()
+
     barrier = pltpu.get_barrier_semaphore()
     has_left, has_right = me > 0, me < n - 1
 
@@ -299,7 +318,7 @@
     pl.semaphore_wait(barrier, has_left.astype(jnp.int32) + has_right.astype(jnp.int32))
 
     def rim_copy(which):
-        source, target = ((x_ref, rim_x), (maps_ref, rim_maps))[which]
+        source, target = ((x_hbm, rim_x), (maps_hbm, rim_maps))[which]
         return pltpu.make_async_remote_copy(
             src_ref=source.at[pl.ds(length - rim, rim)],
             dst_ref=target,
@@ -313,6 +332,9 @@
     def _():
         for which in range(2):
             rim_copy(which).start()
+
+    for load in loads:
+        load.wait()
 
     @pl.when(has_left)
     def _():
@@ -355,6 +377,38 @@
     end_weight = jnp.exp(cum[length - 1 : length] - cum) * step_ref[...]
     grown = jnp.exp(cum)
 
+    late = me >= n // 2
+
+    def chain_copy(c):
+        return pltpu.make_async_remote_copy(
+            src_ref=leaving.at[c],
+            dst_ref=arrived.at[c],
+            send_sem=chain_send.at[c],
+            recv_sem=chain_recv.at[c],
+            device_id=(me + 1, z),
+            device_id_type=mesh_ids,
+        )
+
+    def link(c, carry):
+        span = pl.ds(pl.multiple_of(c * tile, tile), tile)
+
+        @pl.when(has_left)
+        def _():
+            chain_copy(c).wait_recv()
+
+        @pl.when(jnp.logical_not(has_left))
+        def _():
+            arrived[c] = jnp.zeros_like(arrived[c])
+
+        @pl.when(has_right)
+        def _():
+            leaving[c] = (
+                decay_ref[:, span] * arrived[c].astype(jnp.float32) + local[c]
+            ).astype(jnp.bfloat16)
+            chain_copy(c).start()
+
+        return carry
+
     def states(c, carry):
         start = pl.multiple_of(c * tile, tile)
         span = pl.ds(start, tile)
@@ -365,39 +419,14 @@
         local[c] = lax.dot_general(
             b_maps[g], weighted, (((0,), (0,)), ((), ())), preferred_element_type=jnp.float32
         )
+
+        @pl.when(jnp.logical_not(late))
+        def _():
+            link(c, 0)
+
         return carry
 
     lax.fori_loop(0, tiles, states, 0)
-
-    def chain_copy(c):
-        return pltpu.make_async_remote_copy(
-            src_ref=leaving.at[c],
-            dst_ref=arrived.at[c],
-            send_sem=chain_send.at[c],
-            recv_sem=chain_recv.at[c],
-            device_id=(me + 1, z),
-            device_id_type=mesh_ids,
-        )
-
-    def link(c, carry):
-        span = pl.ds(pl.multiple_of(c * tile, tile), tile)
-
-        @pl.when(has_left)
-        def _():
-            chain_copy(c).wait_recv()
-
-        @pl.when(jnp.logical_not(has_left))
-        def _():
-            arrived[c] = jnp.zeros_like(arrived[c])
-
-        @pl.when(has_right)
-        def _():
-            leaving[c] = (
-                decay_ref[:, span] * arrived[c].astype(jnp.float32) + local[c]
-            ).astype(jnp.bfloat16)
-            chain_copy(c).start()
-
-        return carry
 
     pair = 2 * HEAD_DIM
     causal = lax.broadcasted_iota(jnp.int32, (length, length), 0) >= lax.broadcasted_iota(
@@ -423,20 +452,11 @@
         y[:, span] = jnp.where(first, sums[0], sums[1])
         return carry
 
-    late = me >= n // 2
-
-    def phase(turn, carry):
-        @pl.when((turn == 0) == late)
-        def _():
-            lax.fori_loop(0, channels // pair, within, 0)
-
-        @pl.when(turn == 0)
-        def _():
-            lax.fori_loop(0, tiles, link, 0)
-
-        return carry
-
-    lax.fori_loop(0, 2, phase, 0)
+    lax.fori_loop(0, channels // pair, within, 0)
+
+    @pl.when(late)
+    def _():
+        lax.fori_loop(0, tiles, link, 0)
 
     for g in range(groups_here):
         per = group_width // tile
@@ -493,15 +513,19 @@
     decay = jnp.repeat(jnp.exp(cum[-1]), HEAD_DIM)[None]
     skips = jnp.repeat(skip, HEAD_DIM)[None]
     operands = (
-        x, gate, maps, cum, cum.T, step, step.T, decay, skips,
-        taps, base[None], map_taps, map_base[None], gain[None],
+        x, gate, maps, taps, base[None], map_taps, map_base[None], gain[None],
+        cum, cum.T, step, step.T, decay, skips,
     )
+    loaded = operands[:8]
     return pl.pallas_call(
         functools.partial(front_kernel, n, per_group, whole_groups),
         out_shape=jax.ShapeDtypeStruct((length, channels), bf16 if whole_groups else f32),
-        in_specs=[vmem] * len(operands),
+        in_specs=[pl.BlockSpec(memory_space=pltpu.HBM)] * len(loaded)
+        + [vmem] * (len(operands) - len(loaded)),
         out_specs=vmem,
-        scratch_shapes=[
+        scratch_shapes=[pltpu.VMEM(array.shape, array.dtype) for array in loaded]
+        + [
+            dma((len(loaded),)),
             pltpu.VMEM((rim, channels), bf16),
             pltpu.VMEM((rim, maps.shape[1]), bf16),
             pltpu.VMEM((rim + length, max(tile, STATE)), f32),

time: 130 us -> 130 us (level)
  no operation moved by 1% of the time
where the time goes in v3:
time: 130 us
  Pallas kernels  116 us (89%)
  local copies, waits for them, and re-layouts  10 us (8%)
  other arithmetic  3.92 us (3%)
    pallas_call x1, Pallas kernels, mix(): pl.pallas_call(functools.partial(mix_kernel, n, m), out_shape=jax.ShapeDt...  98.9 us
    pallas_call x1, Pallas kernels, front(): pl.pallas_call(functools.partial(front_kernel, n, per_group, whole_groups...  16.7 us
    unnamed x18, local copies, waits for them, and re-layouts  8.25 us

profile of v3, /device:TPU:0, one launch (start us, length us, event | category | flops | bytes accessed | tf_op | source)
XLA Modules:
  0.0 129.7 jit_solution(256524581469649662)
XLA Ops:
  0.0 0.7 exponential_negate_fusion
  0.7 0.7 broadcast_in_dim.20
  1.4 0.1 broadcast_in_dim_reshape.7.skip_ref
  1.5 0.8 fusion.2
  2.3 0.6 reduce-window.6
  2.9 0.2 slice_reduce_fusion
  3.1 0.1 copy_bitcast_fusion
  3.2 0.2 fusion
  3.4 0.1 broadcast_in_dim.19
  3.4 0.1 broadcast_in_dim_reshape.6.decay_ref
  3.5 0.1 copy.20.cum_ref
  3.6 0.1 copy.21.step_ref
  3.7 0.0 copy-start
  3.7 1.2 copy-done
  5.0 0.0 copy-start.1
  5.0 1.2 copy-done.1
  6.2 0.0 copy-start.2
  6.2 1.2 copy-done.2
  7.4 0.0 copy-start.3
  7.4 0.8 copy-done.3
  8.2 0.0 copy-start.4
  8.2 0.8 copy-done.4
  8.9 0.0 copy-start.5
  8.9 0.7 copy-done.5
  9.6 0.0 copy-start.6
  9.6 0.7 copy-done.6
  10.3 0.0 copy-start.7
  10.3 0.7 copy-done.7
  11.0 16.7 %shard_map.127.x_ref = bf16[256,2048]{1,0:T(8,128)(2,1)S(1)} custom-call(bf16[256,2048]{1,0:T(8,128)(2,1)S(1)} %copy-done, bf16[256,2048]{1,0:T(8,128)(2,1)S(1)} %copy-done.1, bf16[256,2048]{1,0:T(8,128)(2,1)S(1)} %copy-done.2, f32[4,2048]{1,0:T(4,128)S(1)} %copy-done.3, f32[1,2048]{1,0:T(1,128)S(1)} %bitcast.24, f32[4,2048]{1,0:T(4,128)S(1)} %copy-done.4, ...), custom_call_target="tpu_custom_call" | custom-call | tf_op jit(solution)/shard_map/pallas_call | solution.py:520
  27.8 98.9 %shard_map.128 = bf16[8,64,1024]{2,1,0:T(8,128)(2,1)S(1)} custom-call(bf16[256,2048]{1,0:T(8,128)(2,1)S(1)} %shard_map.127.x_ref, bf16[2048,1024]{1,0:T(8,128)(2,1)} %w_ref.1), custom_call_target="tpu_custom_call" | custom-call | flops 8589934592 | bytes 5242880 | tf_op jit(solution)/shard_map/pallas_call | solution.py:239
  126.7 0.2 convert_bitcast_fusion
  127.0 0.0 copy-start.8
  127.0 0.2 copy.25
  127.2 1.0 copy-done.8
  128.2 1.5 %convert_add_fusion = f32[64,8192]{1,0:T(8,128)} fusion(f32[64,8192]{1,0:T(8,128)S(1)} %bitcast.27, bf16[64,8192]{1,0:T(8,128)(2,1)S(1)} %copy-done.8), kind=kLoop, calls=%fused_computation.1 | loop fusion | flops 1048576 | bytes 5242880 | tf_op jit(solution)/shard_map/add | solution.py:591
  (3 shorter events, 0.0 us)
Async XLA Ops:
  3.7 1.2 copy-start
  5.0 1.2 copy-start.1
  6.2 1.2 copy-start.2
  7.4 0.8 copy-start.3
  8.2 0.8 copy-start.4
  8.9 0.7 copy-start.5
  9.6 0.7 copy-start.6
  10.3 0.7 copy-start.7
  127.0 1.2 copy-start.8
